TPU v7x, 512 devices: a whole 4x8x8 slice. The times are simulated.
512 devices in a mesh: ctx: 16 (over z, core), tis: 8 (over y), rep: 4 (over x).
Axes of the slice: x: 4, y: 8, z: 8, core: 2. Of those that a mesh axis runs over, the one named last changes fastest.
Arguments:
- donor_feat: bfloat16 [4, 256, 256], P('rep', 'ctx'), may hold values from -6 to 6
- acceptor_feat: bfloat16 [4, 256, 256], P('rep', 'ctx'), may hold values from -6 to 6
- donor_pos: int32 [4, 256], P('rep', 'ctx'), may hold values from 0 to 65535
- acceptor_pos: int32 [4, 256], P('rep'), may hold values from 0 to 65535
- pair_mask: int32 [4, 256, 80], P('rep', 'ctx'), may hold values from 0 to 1
- targets: int32 [4, 256, 32], P('rep', 'ctx', 'tis'), may hold values from 0 to 80, as said below
- dist_table: bfloat16 [128, 256], replicated, may hold values from -3 to 3
- hidden_weights: bfloat16 [32, 256, 512], P('tis'), may hold values from -0.375 to 0.375
- output_weights: bfloat16 [32, 512], P('tis')
Outputs:
- donor_loss: float32 [4, 256, 32], P('rep', 'ctx', 'tis')
- grad_hidden: float32 [32, 256, 512], P('tis', ('ctx', 'rep'))
- grad_acceptor: float32 [4, 256, 256], P('rep', 'ctx')
Inputs may be any that keep to these rules, and one draw needn't show every extreme that they name: `targets`: each target is a valid slot of its donor, or 80 for no splice.
All inputs are finite; a program needn't handle non-finite values.
Results may differ from a plain program's by a relative error of at most 0.002.
The roundings to bfloat16 on the way count: a program that leaves them out, or rounds other values in their place, can miss the bound.
Values may be sent and summed in bfloat16 or wider, within the bound.
A program may use at most 64 MiB of HBM per device.

v0:
```python
import jax
import jax.numpy as jnp
from jax import lax
from jax.sharding import PartitionSpec as P

BLOCK_BP = 65536
SPAN_BLOCKS = 4
BIN_BP = 2048
BINS = 128


def passed_along(value, axis, steps):
    count = lax.axis_size(axis)
    first, last = (max(0, -steps), min(count, count - steps))
    return lax.ppermute(value, axis, [(source, source + steps) for source in range(first, last)])


def silu_grad(values):
    sig = jax.nn.sigmoid(values)
    return sig * (1.0 + values * (1.0 - sig))


def on_device(
    donor_feat,
    acceptor_feat,
    donor_pos,
    acceptor_pos,
    pair_mask,
    targets,
    dist_table,
    hidden_weights,
    output_weights,
):
    seq_dev, don_blk, width = donor_feat.shape
    acc_blk = acceptor_feat.shape[1]
    blocks = lax.axis_size("ctx")
    reach = SPAN_BLOCKS + 1
    slots = reach * acc_blk
    here = lax.axis_index("ctx")
    pieces = [acceptor_feat]
    current = acceptor_feat
    for offset in range(1, reach):
        current = passed_along(current, "ctx", -1)
        pieces.append(current)
    window = jnp.stack(pieces, axis=1).reshape(seq_dev, slots, width)
    pos_pad = jnp.concatenate(
        [acceptor_pos, jnp.zeros((seq_dev, SPAN_BLOCKS * acc_blk), jnp.int32)], axis=1
    )
    pos_win = lax.dynamic_slice_in_dim(pos_pad, here * acc_blk, slots, 1)
    slot_block = jnp.arange(slots, dtype=jnp.int32) // acc_blk
    inchain = here + slot_block < blocks
    dist = slot_block * BLOCK_BP + pos_win[:, None, :] - donor_pos[:, :, None]
    valid = (pair_mask > 0) & (dist > 0) & (dist <= SPAN_BLOCKS * BLOCK_BP) & inchain[None, None, :]
    bins = jnp.clip((dist - 1) // BIN_BP, 0, BINS - 1)
    lookup = (
        (bins[..., None] == jnp.arange(BINS, dtype=jnp.int32))
        .astype(jnp.bfloat16)
        .reshape(-1, BINS)
    )
    table = jnp.dot(lookup, dist_table, preferred_element_type=jnp.float32).reshape(
        seq_dev, don_blk, slots, width
    )
    pre = (
        donor_feat.astype(jnp.float32)[:, :, None, :] + window.astype(jnp.float32)[:, None] + table
    )
    flat = jax.nn.silu(pre).astype(jnp.bfloat16).reshape(-1, width)
    grad_pair = jnp.zeros((flat.shape[0], width), jnp.float32)
    losses = []
    fulls = []
    slot_ids = jnp.arange(slots, dtype=jnp.int32)
    for tissue in range(hidden_weights.shape[0]):
        w_in = hidden_weights[tissue]
        w_out = output_weights[tissue]
        goal = targets[:, :, tissue]
        hid = jnp.dot(flat, w_in, preferred_element_type=jnp.float32)
        act = jax.nn.silu(hid).astype(jnp.bfloat16)
        logits = jnp.dot(act, w_out, preferred_element_type=jnp.float32).reshape(
            seq_dev, don_blk, slots
        )
        masked = jnp.where(valid, logits, -jnp.inf)
        top = jnp.maximum(jnp.max(masked, axis=-1), 0.0)
        expo = jnp.exp(masked - top[..., None])
        total = jnp.sum(expo, axis=-1) + jnp.exp(-top)
        picked = jnp.take_along_axis(logits, jnp.minimum(goal, slots - 1)[..., None], axis=-1)[
            ..., 0
        ]
        picked = jnp.where(goal == slots, 0.0, picked)
        losses.append(top + jnp.log(total) - picked)
        onehot = (goal[..., None] == slot_ids).astype(jnp.float32)
        grad_logits = expo / total[..., None] - onehot
        grad_act = grad_logits.reshape(-1)[:, None] * w_out.astype(jnp.float32)[None, :]
        grad_hid = (grad_act * silu_grad(hid)).astype(jnp.bfloat16)
        grad_pair = grad_pair + lax.dot_general(
            grad_hid, w_in, (((1,), (1,)), ((), ())), preferred_element_type=jnp.float32
        )
        fulls.append(
            lax.dot_general(
                flat, grad_hid, (((0,), (0,)), ((), ())), preferred_element_type=jnp.float32
            )
        )
    stacked = jnp.stack(fulls, axis=1)
    grad_hidden = jnp.transpose(
        lax.psum_scatter(stacked, ("ctx", "rep"), scatter_dimension=0, tiled=True), (1, 0, 2)
    )
    grad_pre = grad_pair.reshape(seq_dev, don_blk, slots, width) * silu_grad(pre)
    contrib = jnp.sum(grad_pre, axis=1).reshape(seq_dev, reach, acc_blk, width)
    carried = contrib[:, reach - 1]
    for offset in range(reach - 2, -1, -1):
        carried = passed_along(carried, "ctx", 1) + contrib[:, offset]
    grad_acceptor = lax.psum(carried, "tis")
    donor_loss = jnp.stack(losses, axis=-1)
    return (donor_loss, grad_hidden, grad_acceptor)


def solution(mesh):
    placed = (
        P("rep", "ctx", None),
        P("rep", "ctx", None),
        P("rep", "ctx"),
        P("rep", None),
        P("rep", "ctx", None),
        P("rep", "ctx", "tis"),
        P(),
        P("tis", None, None),
        P("tis", None),
    )
    return jax.shard_map(
        on_device,
        mesh=mesh,
        in_specs=placed,
        out_specs=(P("rep", "ctx", "tis"), P("tis", ("ctx", "rep"), None), P("rep", "ctx", None)),
        check_vma=False,
    )
```

profile of v0, /device:TPU:8, one launch (start us, length us, event | category | flops | bytes accessed | tf_op | source)
XLA Modules:
  0.0 280.9 jit_solution(4810384354852864490)
XLA Ops:
  7.2 1.3 collective-permute-start
  9.9 0.8 slice_bitcast_fusion.8
  10.8 0.9 slice_reduce_fusion.3
  13.2 1.3 collective-permute-start.1
  14.6 2.4 collective-permute-done.1
  16.9 1.3 collective-permute-start.2
  18.2 3.9 %collective-permute-done.2 = bf16[1,16,256]{2,1,0:T(8,128)(2,1)S(1)} collective-permute-done((bf16[1,16,256]{2,1,0:T(8,128)(2,1)S(1)}, bf16[1,16,256]{2,1,0:T(8,128)(2,1)S(1)}, u32[]{:S(2)}, u32[]{:S(2)}) %collective-permute-start.2) | collective-permute-done | bytes 8224 | tf_op jit(solution)/shard_map/ppermute | solution.py:15
  22.2 1.3 collective-permute-start.3
  23.5 3.7 %collective-permute-done.3 = bf16[1,16,256]{2,1,0:T(8,128)(2,1)S(1)} collective-permute-done((bf16[1,16,256]{2,1,0:T(8,128)(2,1)S(1)}, bf16[1,16,256]{2,1,0:T(8,128)(2,1)S(1)}, u32[]{:S(2)}, u32[]{:S(2)}) %collective-permute-start.3) | collective-permute-done | bytes 8224 | tf_op jit(solution)/shard_map/ppermute | solution.py:15
  27.2 1.7 multiply_convert_fusion.8
  28.9 0.9 multiply_convert_fusion.7
  29.7 2.3 multiply_convert_fusion.4
  32.0 2.3 multiply_convert_fusion.5
  34.3 2.3 multiply_convert_fusion.6
  39.5 1.0 multiply_convert_fusion.3
  40.5 1.4 convolution_bitcast_fusion.3
  41.9 2.5 fusion.10
  44.5 2.7 multiply_convert_fusion
  47.2 1.3 convolution_bitcast_fusion
  48.6 2.7 multiply_convert_fusion.1
  51.3 1.3 convolution_bitcast_fusion.1
  52.8 2.7 multiply_convert_fusion.2
  60.1 4.3 %collective-permute-start.4 = (f32[1,16,256]{2,1,0:T(8,128)S(1)}, f32[1,16,256]{2,1,0:T(8,128)S(1)}, u32[]{:S(2)}, u32[]{:S(2)}) collective-permute-start(f32[1,16,256]{2,1,0:T(8,128)S(1)} %slice_bitcast_fusion.4), channel_id=1, source_target_pairs={{0,32},{32,64},{64,96},{96,128},{128,160},{160,192},{192,224},{224... | collective-permute-start | bytes 49160 | tf_op jit(solution)/shard_map/ppermute | solution.py:15
  64.5 1.5 pad_maximum_fusion
  66.0 2.0 collective-permute-start.5
  68.0 1.3 dynamic-slice
  72.6 4.3 %collective-permute-start.6 = (f32[1,16,256]{2,1,0:T(8,128)S(1)}, f32[1,16,256]{2,1,0:T(8,128)S(1)}, u32[]{:S(2)}, u32[]{:S(2)}) collective-permute-start(f32[1,16,256]{2,1,0:T(8,128)S(1)} %fusion.25), channel_id=1, source_target_pairs={{0,32},{32,64},{64,96},{96,128},{128,160},{160,192},{192,224},{224... | collective-permute-start | bytes 49160 | tf_op jit(solution)/shard_map/ppermute | solution.py:15
  77.0 0.8 collective-permute-done.6
  77.8 2.2 collective-permute-start.7
  80.8 30.4 %psum.7 = f32[1,16,256]{2,1,0:T(8,128)} all-reduce(f32[1,16,256]{2,1,0:T(8,128)S(1)} %fusion.23), channel_id=1, replica_groups=mesh['ctx'=16,'tis'=8,'rep'=4] {'tis'}, use_global_device_ids=true, to_apply=%region_10.12 | all-reduce | flops 4096 | bytes 32768 | tf_op jit(solution)/shard_map/psum | solution.py:110
  111.2 161.4 %all-reduce.4.cloned.1.call-done = f32[256,4,512]{2,0,1:T(8,128)} async-done(((f32[256,4,512]{2,0,1:T(8,128)}), f32[256,4,512]{2,0,1:T(8,128)}) %all-reduce.4.cloned.1.call-update) | async-done | bytes 2097168
  272.6 1.5 dynamic-slice_bitcast_fusion
  (81 shorter events, 14.2 us)
Async XLA Ops:
  7.2 20.0 %copy-start = (bf16[128,256]{1,0:T(8,128)(2,1)S(1)}, bf16[128,256]{1,0:T(8,128)(2,1)}, u32[]{:S(2)}) copy-start(bf16[128,256]{1,0:T(8,128)(2,1)} %param.17) | copy-start | bytes 196612
  7.2 265.4 %all-reduce.4.cloned.1.call-start = ((), (), s32[]{:S(2)}) async-start(), calls=%async_computation | async-start | bytes 4194304
  7.2 6.0 %collective-permute-start = (bf16[1,16,256]{2,1,0:T(8,128)(2,1)}, bf16[1,16,256]{2,1,0:T(8,128)(2,1)S(1)}, u32[]{:S(2)}, u32[]{:S(2)}) collective-permute-start(bf16[1,16,256]{2,1,0:T(8,128)(2,1)} %param.12), channel_id=1, source_target_pairs={{32,0},{64,32},{96,64},{128,96},{160,128},{192,160},{224,192},{256... | collective-permute-start | bytes 24584 | tf_op jit(solution)/shard_map/ppermute | solution.py:15
  13.2 3.7 %collective-permute-start.1 = (bf16[1,16,256]{2,1,0:T(8,128)(2,1)S(1)}, bf16[1,16,256]{2,1,0:T(8,128)(2,1)S(1)}, u32[]{:S(2)}, u32[]{:S(2)}) collective-permute-start(bf16[1,16,256]{2,1,0:T(8,128)(2,1)S(1)} %collective-permute-done), channel_id=1, source_target_pairs={{32,0},{64,32},{96,64},{128,96},{160,128},{192,160},{224,192},{256... | collective-permute-start | bytes 24584 | tf_op jit(solution)/shard_map/ppermute | solution.py:15
  16.9 5.2 %collective-permute-start.2 = (bf16[1,16,256]{2,1,0:T(8,128)(2,1)S(1)}, bf16[1,16,256]{2,1,0:T(8,128)(2,1)S(1)}, u32[]{:S(2)}, u32[]{:S(2)}) collective-permute-start(bf16[1,16,256]{2,1,0:T(8,128)(2,1)S(1)} %collective-permute-done.1), channel_id=1, source_target_pairs={{32,0},{64,32},{96,64},{128,96},{160,128},{192,160},{224,192},{256... | collective-permute-start | bytes 24584 | tf_op jit(solution)/shard_map/ppermute | solution.py:15
  22.2 5.0 %collective-permute-start.3 = (bf16[1,16,256]{2,1,0:T(8,128)(2,1)S(1)}, bf16[1,16,256]{2,1,0:T(8,128)(2,1)S(1)}, u32[]{:S(2)}, u32[]{:S(2)}) collective-permute-start(bf16[1,16,256]{2,1,0:T(8,128)(2,1)S(1)} %collective-permute-done.2), channel_id=1, source_target_pairs={{32,0},{64,32},{96,64},{128,96},{160,128},{192,160},{224,192},{256... | collective-permute-start | bytes 24584 | tf_op jit(solution)/shard_map/ppermute | solution.py:15
  27.1 1.7 copy-start.6
  34.3 2.3 copy-start.8
  37.1 1.7 copy-start.10
  37.2 1.7 copy-start.11
  55.5 1.3 copy-start.1
  55.5 1.6 copy-start.7
  58.3 1.3 copy-start.5
  58.9 5.6 %copy-start.2 = (f32[256,1,512]{2,0,1:T(8,128)S(1)}, f32[256,1,512]{2,0,1:T(8,128)}, u32[]{:S(2)}) copy-start(f32[256,1,512]{2,0,1:T(8,128)} %convolution_bitcast_fusion.3) | copy-start | bytes 1572868
  58.9 5.6 %copy-start.3 = (f32[256,1,512]{2,0,1:T(8,128)S(1)}, f32[256,1,512]{2,0,1:T(8,128)}, u32[]{:S(2)}) copy-start(f32[256,1,512]{2,0,1:T(8,128)} %convolution_bitcast_fusion) | copy-start | bytes 1572868
  58.9 5.6 %copy-start.4 = (f32[256,1,512]{2,0,1:T(8,128)S(1)}, f32[256,1,512]{2,0,1:T(8,128)}, u32[]{:S(2)}) copy-start(f32[256,1,512]{2,0,1:T(8,128)} %convolution_bitcast_fusion.1) | copy-start | bytes 1572868
  60.1 5.8 %collective-permute-start.4 = (f32[1,16,256]{2,1,0:T(8,128)S(1)}, f32[1,16,256]{2,1,0:T(8,128)S(1)}, u32[]{:S(2)}, u32[]{:S(2)}) collective-permute-start(f32[1,16,256]{2,1,0:T(8,128)S(1)} %slice_bitcast_fusion.4), channel_id=1, source_target_pairs={{0,32},{32,64},{64,96},{96,128},{128,160},{160,192},{192,224},{224... | collective-permute-start | bytes 49160 | tf_op jit(solution)/shard_map/ppermute | solution.py:15
  66.0 11.0 %copy-start.9 = (s32[1,16,4]{1,2,0:T(4,128)S(1)}, s32[1,16,4]{1,2,0:T(4,128)}, u32[]{:S(2)}) copy-start(s32[1,16,4]{1,2,0:T(4,128)} %param.16) | copy-start | bytes 772
  66.0 6.6 %collective-permute-start.5 = (f32[1,16,256]{2,1,0:T(8,128)S(1)}, f32[1,16,256]{2,1,0:T(8,128)S(1)}, u32[]{:S(2)}, u32[]{:S(2)}) collective-permute-start(f32[1,16,256]{2,1,0:T(8,128)S(1)} %fusion.26), channel_id=1, source_target_pairs={{0,32},{32,64},{64,96},{96,128},{128,160},{160,192},{192,224},{224... | collective-permute-start | bytes 49160 | tf_op jit(solution)/shard_map/ppermute | solution.py:15
  72.6 5.1 %collective-permute-start.6 = (f32[1,16,256]{2,1,0:T(8,128)S(1)}, f32[1,16,256]{2,1,0:T(8,128)S(1)}, u32[]{:S(2)}, u32[]{:S(2)}) collective-permute-start(f32[1,16,256]{2,1,0:T(8,128)S(1)} %fusion.25), channel_id=1, source_target_pairs={{0,32},{32,64},{64,96},{96,128},{128,160},{160,192},{192,224},{224... | collective-permute-start | bytes 49160 | tf_op jit(solution)/shard_map/ppermute | solution.py:15
  77.8 3.1 %collective-permute-start.7 = (f32[1,16,256]{2,1,0:T(8,128)S(1)}, f32[1,16,256]{2,1,0:T(8,128)S(1)}, u32[]{:S(2)}, u32[]{:S(2)}) collective-permute-start(f32[1,16,256]{2,1,0:T(8,128)S(1)} %fusion.24), channel_id=1, source_target_pairs={{0,32},{32,64},{64,96},{96,128},{128,160},{160,192},{192,224},{224... | collective-permute-start | bytes 49160 | tf_op jit(solution)/shard_map/ppermute | solution.py:15
Sparse Core Ops, SparseCore 0:
  66.1 206.4 all-reduce.3
where the time goes:
time: 282 us; the launch traced here: 281 us
  waiting for transfers between devices  172 us (61%)
  blocking collectives  30.4 us (11%)
  matrix products  20.5 us (7%)
  starting transfers between devices  18 us (6%)
  other arithmetic  15.4 us (5%)
  between operations  15.1 us (5%)
  local copies, waits for them, and re-layouts  9.11 us (3%)
    unnamed x2, waiting for transfers between devices  161 us
    psum x1, blocking collectives, on_device(): grad_acceptor = lax.psum(carried, 'tis')  30.4 us
    ppermute x8, starting transfers between devices, passed_along(): lax.ppermute(value, axis, [(source, source + steps) for source in range(f...  18 us
    ppermute x8, waiting for transfers between devices, passed_along(): lax.ppermute(value, axis, [(source, source + steps) for source in range(f...  11 us
    convert_element_type x4, other arithmetic, on_device(): grad_hid = (grad_act * silu_grad(hid)).astype(jnp.bfloat16)  9.15 us
    dot_general x4, matrix products, on_device(): hid = jnp.dot(flat, w_in, preferred_element_type=jnp.float32)  7.74 us
  transfers between devices with their start and end apart: 9, of which 6 were waited for; matrix products, arithmetic and copies ran while one was open for 4% of the time, Pallas kernels for 0%

commit v1 on v0

--- a/solution.py
+++ b/solution.py
@@ -107,7 +107,8 @@
     carried = contrib[:, reach - 1]
     for offset in range(reach - 2, -1, -1):
         carried = passed_along(carried, "ctx", 1) + contrib[:, offset]
-    grad_acceptor = lax.psum(carried, "tis")
+    parts = lax.all_gather(carried, "tis", axis=0, tiled=False)
+    grad_acceptor = parts.sum(axis=0)
     donor_loss = jnp.stack(losses, axis=-1)
     return (donor_loss, grad_hidden, grad_acceptor)
 

time: 282 us -> 292 us (1.035)
  waiting for transfers between devices: 172 us -> 184 us
  blocking collectives: 30.4 us -> 26.8 us
    psum x1 -> x0, blocking collectives: 30.4 us -> none  [on_device(): grad_acceptor = lax.psum(carried, 'tis')]
    all_gather x0 -> x1, blocking collectives: none -> 26.8 us  [on_device(): parts = lax.all_gather(carried, 'tis', axis=0, tiled=False)]
    unnamed x2, waiting for transfers between devices: 161 us -> 172 us
  transfers between devices with their start and end apart: 9 -> 9, of which waited for: 6 -> 7; matrix products, arithmetic and copies ran while one was open for 4% -> 4% of each run, Pallas kernels for 0% -> 0%
where the time goes in v1:
time: 292 us; the launch traced here: 291 us
  waiting for transfers between devices  184 us (63%)
  blocking collectives  26.8 us (9%)
  matrix products  19.8 us (7%)
  starting transfers between devices  18 us (6%)
  other arithmetic  17.9 us (6%)
  between operations  15.1 us (5%)
  local copies, waits for them, and re-layouts  9.92 us (3%)
    unnamed x2, waiting for transfers between devices  172 us
    all_gather x1, blocking collectives, on_device(): parts = lax.all_gather(carried, 'tis', axis=0, tiled=False)  26.8 us
    ppermute x8, starting transfers between devices, passed_along(): lax.ppermute(value, axis, [(source, source + steps) for source in range(f...  18 us
    ppermute x8, waiting for transfers between devices, passed_along(): lax.ppermute(value, axis, [(source, source + steps) for source in range(f...  11.3 us
    convert_element_type x4, other arithmetic, on_device(): grad_hid = (grad_act * silu_grad(hid)).astype(jnp.bfloat16)  11 us
    dot_general x4, matrix products, on_device(): hid = jnp.dot(flat, w_in, preferred_element_type=jnp.float32)  9.21 us
  transfers between devices with their start and end apart: 9, of which 7 were waited for; matrix products, arithmetic and copies ran while one was open for 4% of the time, Pallas kernels for 0%

profile of v1, /device:TPU:8, one launch (start us, length us, event | category | flops | bytes accessed | tf_op | source)
XLA Modules:
  0.0 291.2 jit_solution(10986963086269245836)
XLA Ops:
  7.2 1.3 collective-permute-start
  9.9 0.8 slice_bitcast_fusion.8
  10.8 0.9 slice_reduce_fusion.3
  13.3 1.3 dynamic-slice
  15.2 1.3 collective-permute-start.1
  16.5 2.4 collective-permute-done.1
  18.9 1.3 collective-permute-start.2
  20.2 3.9 %collective-permute-done.2 = bf16[1,16,256]{2,1,0:T(8,128)(2,1)S(1)} collective-permute-done((bf16[1,16,256]{2,1,0:T(8,128)(2,1)S(1)}, bf16[1,16,256]{2,1,0:T(8,128)(2,1)S(1)}, u32[]{:S(2)}, u32[]{:S(2)}) %collective-permute-start.2) | collective-permute-done | bytes 8224 | tf_op jit(solution)/shard_map/ppermute | solution.py:15
  24.1 1.3 collective-permute-start.3
  25.4 3.7 %collective-permute-done.3 = bf16[1,16,256]{2,1,0:T(8,128)(2,1)S(1)} collective-permute-done((bf16[1,16,256]{2,1,0:T(8,128)(2,1)S(1)}, bf16[1,16,256]{2,1,0:T(8,128)(2,1)S(1)}, u32[]{:S(2)}, u32[]{:S(2)}) %collective-permute-start.3) | collective-permute-done | bytes 8224 | tf_op jit(solution)/shard_map/ppermute | solution.py:15
  29.1 1.6 multiply_convert_fusion.8
  30.7 2.3 multiply_convert_fusion.7
  33.0 2.3 multiply_convert_fusion.4
  35.3 2.3 multiply_convert_fusion.5
  37.6 2.3 multiply_convert_fusion.6
  42.9 2.7 multiply_convert_fusion
  45.6 1.3 convolution_bitcast_fusion
  47.0 2.7 multiply_convert_fusion.1
  49.7 1.4 convolution_bitcast_fusion.1
  51.2 2.7 multiply_convert_fusion.2
  53.9 1.1 copy-done.1
  55.0 1.4 convolution_bitcast_fusion.2
  56.5 2.8 multiply_convert_fusion.3
  63.5 4.3 %collective-permute-start.4 = (f32[1,16,256]{2,1,0:T(8,128)S(1)}, f32[1,16,256]{2,1,0:T(8,128)S(1)}, u32[]{:S(2)}, u32[]{:S(2)}) collective-permute-start(f32[1,16,256]{2,1,0:T(8,128)S(1)} %slice_bitcast_fusion.4), channel_id=1, source_target_pairs={{0,32},{32,64},{64,96},{96,128},{128,160},{160,192},{192,224},{224... | collective-permute-start | bytes 49160 | tf_op jit(solution)/shard_map/ppermute | solution.py:15
  68.7 2.2 collective-permute-start.5
  71.0 1.5 pad_maximum_fusion
  75.1 4.0 %collective-permute-start.6 = (f32[1,16,256]{2,1,0:T(8,128)S(1)}, f32[1,16,256]{2,1,0:T(8,128)S(1)}, u32[]{:S(2)}, u32[]{:S(2)}) collective-permute-start(f32[1,16,256]{2,1,0:T(8,128)S(1)} %fusion.25), channel_id=1, source_target_pairs={{0,32},{32,64},{64,96},{96,128},{128,160},{160,192},{192,224},{224... | collective-permute-start | bytes 49160 | tf_op jit(solution)/shard_map/ppermute | solution.py:15
  79.2 0.8 collective-permute-done.6
  80.0 2.3 collective-permute-start.7
  83.1 26.8 %all-gather = f32[8,16,256]{2,1,0:T(8,128)S(1)} all-gather(f32[1,16,256]{2,1,0:T(8,128)S(1)} %fusion.23), channel_id=2, replica_groups=mesh['ctx'=16,'tis'=8,'rep'=4] {'tis'}, dimensions={0}, use_global_device_ids=true | all-gather | bytes 147456 | tf_op jit(solution)/shard_map/all_gather | solution.py:110
  110.5 172.4 %all-reduce.4.cloned.1.call-done = f32[256,4,512]{2,0,1:T(8,128)} async-done(((f32[256,4,512]{2,0,1:T(8,128)}), f32[256,4,512]{2,0,1:T(8,128)}) %all-reduce.4.cloned.1.call-update) | async-done | bytes 2097168
  282.9 1.5 dynamic-slice_bitcast_fusion
  (84 shorter events, 15.3 us)
Async XLA Ops:
  7.2 21.9 %copy-start = (bf16[128,256]{1,0:T(8,128)(2,1)S(1)}, bf16[128,256]{1,0:T(8,128)(2,1)}, u32[]{:S(2)}) copy-start(bf16[128,256]{1,0:T(8,128)(2,1)} %param.17) | copy-start | bytes 196612
  7.2 275.7 %all-reduce.4.cloned.1.call-start = ((), (), s32[]{:S(2)}) async-start(), calls=%async_computation | async-start | bytes 4194304
  7.2 8.0 %collective-permute-start = (bf16[1,16,256]{2,1,0:T(8,128)(2,1)}, bf16[1,16,256]{2,1,0:T(8,128)(2,1)S(1)}, u32[]{:S(2)}, u32[]{:S(2)}) collective-permute-start(bf16[1,16,256]{2,1,0:T(8,128)(2,1)} %param.12), channel_id=1, source_target_pairs={{32,0},{64,32},{96,64},{128,96},{160,128},{192,160},{224,192},{256... | collective-permute-start | bytes 24584 | tf_op jit(solution)/shard_map/ppermute | solution.py:15
  15.2 3.7 %collective-permute-start.1 = (bf16[1,16,256]{2,1,0:T(8,128)(2,1)S(1)}, bf16[1,16,256]{2,1,0:T(8,128)(2,1)S(1)}, u32[]{:S(2)}, u32[]{:S(2)}) collective-permute-start(bf16[1,16,256]{2,1,0:T(8,128)(2,1)S(1)} %collective-permute-done), channel_id=1, source_target_pairs={{32,0},{64,32},{96,64},{128,96},{160,128},{192,160},{224,192},{256... | collective-permute-start | bytes 24584 | tf_op jit(solution)/shard_map/ppermute | solution.py:15
  18.9 5.2 %collective-permute-start.2 = (bf16[1,16,256]{2,1,0:T(8,128)(2,1)S(1)}, bf16[1,16,256]{2,1,0:T(8,128)(2,1)S(1)}, u32[]{:S(2)}, u32[]{:S(2)}) collective-permute-start(bf16[1,16,256]{2,1,0:T(8,128)(2,1)S(1)} %collective-permute-done.1), channel_id=1, source_target_pairs={{32,0},{64,32},{96,64},{128,96},{160,128},{192,160},{224,192},{256... | collective-permute-start | bytes 24584 | tf_op jit(solution)/shard_map/ppermute | solution.py:15
  24.1 5.0 %collective-permute-start.3 = (bf16[1,16,256]{2,1,0:T(8,128)(2,1)S(1)}, bf16[1,16,256]{2,1,0:T(8,128)(2,1)S(1)}, u32[]{:S(2)}, u32[]{:S(2)}) collective-permute-start(bf16[1,16,256]{2,1,0:T(8,128)(2,1)S(1)} %collective-permute-done.2), channel_id=1, source_target_pairs={{32,0},{64,32},{96,64},{128,96},{160,128},{192,160},{224,192},{256... | collective-permute-start | bytes 24584 | tf_op jit(solution)/shard_map/ppermute | solution.py:15
  29.1 1.6 copy-start.7
  37.6 2.3 copy-start.9
  40.5 1.7 copy-start.11
  40.5 1.7 copy-start.12
  53.9 1.1 copy-start.1
  56.5 2.8 copy-start.8
  59.3 1.3 copy-start.2
  61.7 1.3 copy-start.6
  63.0 7.9 %copy-start.3 = (f32[256,1,512]{2,0,1:T(8,128)S(1)}, f32[256,1,512]{2,0,1:T(8,128)}, u32[]{:S(2)}) copy-start(f32[256,1,512]{2,0,1:T(8,128)} %convolution_bitcast_fusion) | copy-start | bytes 1572868
  63.0 7.9 %copy-start.4 = (f32[256,1,512]{2,0,1:T(8,128)S(1)}, f32[256,1,512]{2,0,1:T(8,128)}, u32[]{:S(2)}) copy-start(f32[256,1,512]{2,0,1:T(8,128)} %convolution_bitcast_fusion.1) | copy-start | bytes 1572868
  63.0 7.9 %copy-start.5 = (f32[256,1,512]{2,0,1:T(8,128)S(1)}, f32[256,1,512]{2,0,1:T(8,128)}, u32[]{:S(2)}) copy-start(f32[256,1,512]{2,0,1:T(8,128)} %convolution_bitcast_fusion.2) | copy-start | bytes 1572868
  63.5 5.2 %collective-permute-start.4 = (f32[1,16,256]{2,1,0:T(8,128)S(1)}, f32[1,16,256]{2,1,0:T(8,128)S(1)}, u32[]{:S(2)}, u32[]{:S(2)}) collective-permute-start(f32[1,16,256]{2,1,0:T(8,128)S(1)} %slice_bitcast_fusion.4), channel_id=1, source_target_pairs={{0,32},{32,64},{64,96},{96,128},{128,160},{160,192},{192,224},{224... | collective-permute-start | bytes 49160 | tf_op jit(solution)/shard_map/ppermute | solution.py:15
  68.7 6.4 %collective-permute-start.5 = (f32[1,16,256]{2,1,0:T(8,128)S(1)}, f32[1,16,256]{2,1,0:T(8,128)S(1)}, u32[]{:S(2)}, u32[]{:S(2)}) collective-permute-start(f32[1,16,256]{2,1,0:T(8,128)S(1)} %fusion.26), channel_id=1, source_target_pairs={{0,32},{32,64},{64,96},{96,128},{128,160},{160,192},{192,224},{224... | collective-permute-start | bytes 49160 | tf_op jit(solution)/shard_map/ppermute | solution.py:15
  72.4 6.7 %copy-start.10 = (s32[1,16,4]{1,2,0:T(4,128)S(1)}, s32[1,16,4]{1,2,0:T(4,128)}, u32[]{:S(2)}) copy-start(s32[1,16,4]{1,2,0:T(4,128)} %param.16) | copy-start | bytes 772
  75.1 4.9 %collective-permute-start.6 = (f32[1,16,256]{2,1,0:T(8,128)S(1)}, f32[1,16,256]{2,1,0:T(8,128)S(1)}, u32[]{:S(2)}, u32[]{:S(2)}) collective-permute-start(f32[1,16,256]{2,1,0:T(8,128)S(1)} %fusion.25), channel_id=1, source_target_pairs={{0,32},{32,64},{64,96},{96,128},{128,160},{160,192},{192,224},{224... | collective-permute-start | bytes 49160 | tf_op jit(solution)/shard_map/ppermute | solution.py:15
  80.0 3.1 %collective-permute-start.7 = (f32[1,16,256]{2,1,0:T(8,128)S(1)}, f32[1,16,256]{2,1,0:T(8,128)S(1)}, u32[]{:S(2)}, u32[]{:S(2)}) collective-permute-start(f32[1,16,256]{2,1,0:T(8,128)S(1)} %fusion.24), channel_id=1, source_target_pairs={{0,32},{32,64},{64,96},{96,128},{128,160},{160,192},{192,224},{224... | collective-permute-start | bytes 49160 | tf_op jit(solution)/shard_map/ppermute | solution.py:15
Sparse Core Ops, SparseCore 0:
  72.6 210.2 all-reduce.3
